TPU v7x, 32 devices: a whole 2x2x4 slice. The times are simulated.
32 devices in a mesh: dom: 16 (over z, y, core), rep: 2 (over x).
Axes of the slice: x: 2, y: 2, z: 4, core: 2. Of those that a mesh axis runs over, the one named last changes fastest.
Arguments:
- features: bfloat16 [4096, 1024], P('dom'), may hold values from -6 to 6
- tiles: bfloat16 [2, 32, 12, 128, 128], P(None, 'dom'), may hold values from 0 to 2, as said below
- columns: int32 [2, 32, 12], P(None, 'dom'), may hold values from 0 to 31, as said below
- counts: int32 [2, 32], P(None, 'dom'), may hold values from 1 to 12, as said below
- degrees: int32 [2, 4096], P(None, 'dom'), may hold values from 16 to 64
- w_self: bfloat16 [1024, 1024], replicated, may hold values from -0.1875 to 0.1875
- w_in: bfloat16 [1024, 1024], replicated, may hold values from -1 to 1
- w_out: bfloat16 [1024, 1024], replicated, may hold values from -1 to 1
Outputs:
- layer_out: bfloat16 [4096, 1024], P('dom')
Inputs may be any that keep to these rules, and one draw needn't show every extreme that they name: Within one block-row the 12 block-columns are distinct; only the first counts slots are read. `counts`: in each relation some block-row has all 12 slots live. `tiles`: edge weights are zero or positive.
All inputs are finite; a program needn't handle non-finite values.
Results may differ from a plain program's by a relative error of at most 0.0038.
Values may be sent and summed in bfloat16 or wider, within the bound.
No kernel may reach another device: no remote copies, remote signals or barrier semaphores. Data moves between devices by JAX's collectives and lax.ppermute only.
A program may use at most 64 MiB of HBM per device.

v0:
```python
import jax
import jax.numpy as jnp
from jax import lax
from jax.sharding import PartitionSpec as P


def from_behind(block, axis, distance):
    devices = range(lax.axis_size(axis))
    route = [((i - distance) % len(devices), i) for i in devices]
    return lax.ppermute(block, axis, route)


def finish(summed, degree_rows, feature_rows, w_self, w_in, w_out):
    scaled = summed / degree_rows[:, :, None].astype(jnp.float32)
    agg_in = scaled[0].astype(jnp.bfloat16)
    agg_out = scaled[1].astype(jnp.bfloat16)
    hidden = jnp.dot(feature_rows, w_self, preferred_element_type=jnp.float32)
    hidden = hidden + jnp.dot(agg_in, w_in, preferred_element_type=jnp.float32)
    hidden = hidden + jnp.dot(agg_out, w_out, preferred_element_type=jnp.float32)
    return jax.nn.relu(hidden).astype(jnp.bfloat16)


def on_device(features, tiles, columns, counts, degrees, w_self, w_in, w_out):
    node_rows, feat_width = features.shape
    tile_size = tiles.shape[3]
    local_blocks = node_rows // tile_size
    cycle_size = lax.axis_size("dom")
    half_cycle = cycle_size // 2
    position = lax.axis_index("dom")
    replica = lax.axis_index("rep")
    slot_ids = jnp.arange(tiles.shape[2], dtype=jnp.int32)
    block_ids = jnp.arange(local_blocks, dtype=jnp.int32)
    live_slots = slot_ids[None, None, :] < counts[:, :, None]

    def absorb(running, feature_panel, source):
        targets = source * local_blocks + block_ids
        matches = (columns[:, :, None, :] == targets[None, None, :, None]) & live_slots[
            :, :, None, :
        ]
        present = jnp.any(matches, axis=-1)
        picks = jnp.sum(jnp.where(matches, slot_ids, 0), axis=-1)
        chosen = jnp.take_along_axis(tiles, picks[:, :, :, None, None], axis=2)
        chosen = jnp.where(present[:, :, :, None, None], chosen, jnp.zeros_like(chosen))
        panel_blocks = feature_panel.reshape(local_blocks, tile_size, feat_width)
        return running + jnp.einsum(
            "ricab,cbh->riah", chosen, panel_blocks, preferred_element_type=jnp.float32
        )

    running = jnp.zeros((2, local_blocks, tile_size, feat_width), jnp.float32)
    distant = from_behind(features, "dom", half_cycle)
    feature_panel = jnp.where(replica == 0, features, distant)
    anchor = (position - replica * half_cycle) % cycle_size

    def advance(turn, carry):
        sums_now, panel_now = carry
        sums_now = absorb(sums_now, panel_now, (anchor - turn) % cycle_size)
        panel_now = from_behind(panel_now, "dom", 1)
        return (sums_now, panel_now)

    running, feature_panel = lax.fori_loop(0, half_cycle - 1, advance, (running, feature_panel))
    running = absorb(running, feature_panel, (anchor - (half_cycle - 1)) % cycle_size)
    stacked = running.reshape(2, node_rows, feat_width)
    summed = lax.psum(stacked, "rep")
    return finish(summed, degrees, features, w_self, w_in, w_out)


def solution(mesh):
    placed = (
        P("dom", None),
        P(None, "dom", None, None, None),
        P(None, "dom", None),
        P(None, "dom"),
        P(None, "dom"),
        P(),
        P(),
        P(),
    )
    return jax.shard_map(
        on_device, mesh=mesh, in_specs=placed, out_specs=P("dom", None), check_vma=False
    )
```

profile of v0, /device:TPU:0, one launch (start us, length us, event | category | flops | bytes accessed | tf_op | source)
XLA Modules:
  0.0 189.8 jit_solution(7590709612621748421)
XLA Ops:
  6.5 4.1 %collective-permute-start.1 = (bf16[256,1024]{1,0:T(8,128)(2,1)}, bf16[256,1024]{1,0:T(8,128)(2,1)S(1)}, u32[]{:S(2)}, u32[]{:S(2)}) collective-permute-start(bf16[256,1024]{1,0:T(8,128)(2,1)} %param.12), channel_id=1, source_target_pairs={{16,0},{18,2},{20,4},{22,6},{24,8},{26,10},{28,12},{30,14},{0,16},... | collective-permute-start | bytes 1572872 | tf_op jit(solution)/shard_map/ppermute | solution.py:10
  12.4 2.7 %gather_fusion.1 = bf16[8,128,128]{2,1,0:T(8,128)(2,1)} fusion(bf16[2,2,12,128,128]{4,3,2,1,0:T(8,128)(2,1)} %param.13, s32[8]{0:T(128)S(1)} %reshape.89), kind=kCustom, calls=%fused_computation.1.clone | custom fusion | bytes 524384 | tf_op jit(solution)/shard_map/jit(take_along_axis)/gather | solution.py:42
  16.0 18.0 %collective-permute-done.1 = bf16[256,1024]{1,0:T(8,128)(2,1)S(1)} collective-permute-done((bf16[256,1024]{1,0:T(8,128)(2,1)}, bf16[256,1024]{1,0:T(8,128)(2,1)S(1)}, u32[]{:S(2)}, u32[]{:S(2)}) %collective-permute-start.1) | collective-permute-done | bytes 524320 | tf_op jit(solution)/shard_map/ppermute | solution.py:10
  34.0 1.1 broadcast_select_fusion
  35.1 79.8 %while.18 = (s32[]{:T(128)}, f32[2,2,128,1024]{3,2,1,0:T(8,128)}, bf16[256,1024]{1,0:T(8,128)(2,1)S(1)}, s32[2,2,12]{2,1,0:T(2,128)S(1)}, s32[]{:T(128)}, /*inde...) while((s32[]{:T(128)}, f32[2,2,128,1024]{3,2,1,0:T(8,128)}, ...), condition=%wide.region_3.5_spmd.clone, body=%wide.region_0.4_spmd.clone.sunk | while | flops 269747040 | bytes 8651944 | solution.py:60
  35.9 2.0 %gather_fusion = bf16[8,128,128]{2,1,0:T(8,128)(2,1)S(1)} fusion(bf16[2,2,12,128,128]{4,3,2,1,0:T(8,128)(2,1)} %get-tuple-element.347, s32[8]{0:T(128)S(1)} %reshape.102), kind=kCustom, calls=%fused_computation.clone.clone.1 | custom fusion | bytes 524384 | tf_op jit(solution)/shard_map/while/body/eval_jaxpr/jit(take_along_axis)/gather | solution.py:42
  37.9 1.8 bitcast_add_fusion.3
  39.8 6.8 %collective-permute-done = bf16[256,1024]{1,0:T(8,128)(2,1)S(1)} collective-permute-done((bf16[256,1024]{1,0:T(8,128)(2,1)S(1)}, bf16[256,1024]{1,0:T(8,128)(2,1)S(1)}, u32[]{:S(2)}, u32[]{:S(2)}) %collective-permute-start) | collective-permute-done | bytes 524320 | tf_op jit(solution)/shard_map/while/body/eval_jaxpr/ppermute | solution.py:10
  47.3 2.0 %gather_fusion = bf16[8,128,128]{2,1,0:T(8,128)(2,1)S(1)} fusion(bf16[2,2,12,128,128]{4,3,2,1,0:T(8,128)(2,1)} %get-tuple-element.347, s32[8]{0:T(128)S(1)} %reshape.102), kind=kCustom, calls=%fused_computation.clone.clone.1 | custom fusion | bytes 524384 | tf_op jit(solution)/shard_map/while/body/eval_jaxpr/jit(take_along_axis)/gather | solution.py:42
  49.3 3.4 %bitcast_add_fusion.3 = f32[2,2,128,1024]{3,2,1,0:T(8,128)} fusion(f32[2,2,128,1024]{3,2,1,0:T(8,128)} %get-tuple-element.331, bf16[2,128,1024,1,1]{2,1,0,4,3:T(8,128)(2,1)S(1)} %bitcast.71, pred[]{:T(512)S(6)} %compare.6, bf16[2,2,2,128,128]{4,3,2,1,0:T(8,128)(2,1)S(1)} %bitcast.72, pred[2,2,2]{2,1,0:T(4,128)(4,1)S(1)} %and_bitcast_fusion.3, ...), kind=kOutput, calls=%fused_computation.5.clone.1 | convolution fusion | flops 269746176 | bytes 4980753 | tf_op jit(solution)/shard_map/while/body/eval_jaxpr/ricab,cbh->riah/dot_general | solution.py:45
  52.8 5.2 %collective-permute-done = bf16[256,1024]{1,0:T(8,128)(2,1)S(1)} collective-permute-done((bf16[256,1024]{1,0:T(8,128)(2,1)S(1)}, bf16[256,1024]{1,0:T(8,128)(2,1)S(1)}, u32[]{:S(2)}, u32[]{:S(2)}) %collective-permute-start) | collective-permute-done | bytes 524320 | tf_op jit(solution)/shard_map/while/body/eval_jaxpr/ppermute | solution.py:10
  58.7 2.0 %gather_fusion = bf16[8,128,128]{2,1,0:T(8,128)(2,1)S(1)} fusion(bf16[2,2,12,128,128]{4,3,2,1,0:T(8,128)(2,1)} %get-tuple-element.347, s32[8]{0:T(128)S(1)} %reshape.102), kind=kCustom, calls=%fused_computation.clone.clone.1 | custom fusion | bytes 524384 | tf_op jit(solution)/shard_map/while/body/eval_jaxpr/jit(take_along_axis)/gather | solution.py:42
  60.7 3.4 %bitcast_add_fusion.3 = f32[2,2,128,1024]{3,2,1,0:T(8,128)} fusion(f32[2,2,128,1024]{3,2,1,0:T(8,128)} %get-tuple-element.331, bf16[2,128,1024,1,1]{2,1,0,4,3:T(8,128)(2,1)S(1)} %bitcast.71, pred[]{:T(512)S(6)} %compare.6, bf16[2,2,2,128,128]{4,3,2,1,0:T(8,128)(2,1)S(1)} %bitcast.72, pred[2,2,2]{2,1,0:T(4,128)(4,1)S(1)} %and_bitcast_fusion.3, ...), kind=kOutput, calls=%fused_computation.5.clone.1 | convolution fusion | flops 269746176 | bytes 4980753 | tf_op jit(solution)/shard_map/while/body/eval_jaxpr/ricab,cbh->riah/dot_general | solution.py:45
  64.2 5.2 %collective-permute-done = bf16[256,1024]{1,0:T(8,128)(2,1)S(1)} collective-permute-done((bf16[256,1024]{1,0:T(8,128)(2,1)S(1)}, bf16[256,1024]{1,0:T(8,128)(2,1)S(1)}, u32[]{:S(2)}, u32[]{:S(2)}) %collective-permute-start) | collective-permute-done | bytes 524320 | tf_op jit(solution)/shard_map/while/body/eval_jaxpr/ppermute | solution.py:10
  70.1 2.0 %gather_fusion = bf16[8,128,128]{2,1,0:T(8,128)(2,1)S(1)} fusion(bf16[2,2,12,128,128]{4,3,2,1,0:T(8,128)(2,1)} %get-tuple-element.347, s32[8]{0:T(128)S(1)} %reshape.102), kind=kCustom, calls=%fused_computation.clone.clone.1 | custom fusion | bytes 524384 | tf_op jit(solution)/shard_map/while/body/eval_jaxpr/jit(take_along_axis)/gather | solution.py:42
  72.1 3.4 %bitcast_add_fusion.3 = f32[2,2,128,1024]{3,2,1,0:T(8,128)} fusion(f32[2,2,128,1024]{3,2,1,0:T(8,128)} %get-tuple-element.331, bf16[2,128,1024,1,1]{2,1,0,4,3:T(8,128)(2,1)S(1)} %bitcast.71, pred[]{:T(512)S(6)} %compare.6, bf16[2,2,2,128,128]{4,3,2,1,0:T(8,128)(2,1)S(1)} %bitcast.72, pred[2,2,2]{2,1,0:T(4,128)(4,1)S(1)} %and_bitcast_fusion.3, ...), kind=kOutput, calls=%fused_computation.5.clone.1 | convolution fusion | flops 269746176 | bytes 4980753 | tf_op jit(solution)/shard_map/while/body/eval_jaxpr/ricab,cbh->riah/dot_general | solution.py:45
  75.6 5.2 %collective-permute-done = bf16[256,1024]{1,0:T(8,128)(2,1)S(1)} collective-permute-done((bf16[256,1024]{1,0:T(8,128)(2,1)S(1)}, bf16[256,1024]{1,0:T(8,128)(2,1)S(1)}, u32[]{:S(2)}, u32[]{:S(2)}) %collective-permute-start) | collective-permute-done | bytes 524320 | tf_op jit(solution)/shard_map/while/body/eval_jaxpr/ppermute | solution.py:10
  81.5 2.0 %gather_fusion = bf16[8,128,128]{2,1,0:T(8,128)(2,1)S(1)} fusion(bf16[2,2,12,128,128]{4,3,2,1,0:T(8,128)(2,1)} %get-tuple-element.347, s32[8]{0:T(128)S(1)} %reshape.102), kind=kCustom, calls=%fused_computation.clone.clone.1 | custom fusion | bytes 524384 | tf_op jit(solution)/shard_map/while/body/eval_jaxpr/jit(take_along_axis)/gather | solution.py:42
  83.5 3.4 %bitcast_add_fusion.3 = f32[2,2,128,1024]{3,2,1,0:T(8,128)} fusion(f32[2,2,128,1024]{3,2,1,0:T(8,128)} %get-tuple-element.331, bf16[2,128,1024,1,1]{2,1,0,4,3:T(8,128)(2,1)S(1)} %bitcast.71, pred[]{:T(512)S(6)} %compare.6, bf16[2,2,2,128,128]{4,3,2,1,0:T(8,128)(2,1)S(1)} %bitcast.72, pred[2,2,2]{2,1,0:T(4,128)(4,1)S(1)} %and_bitcast_fusion.3, ...), kind=kOutput, calls=%fused_computation.5.clone.1 | convolution fusion | flops 269746176 | bytes 4980753 | tf_op jit(solution)/shard_map/while/body/eval_jaxpr/ricab,cbh->riah/dot_general | solution.py:45
  87.0 5.2 %collective-permute-done = bf16[256,1024]{1,0:T(8,128)(2,1)S(1)} collective-permute-done((bf16[256,1024]{1,0:T(8,128)(2,1)S(1)}, bf16[256,1024]{1,0:T(8,128)(2,1)S(1)}, u32[]{:S(2)}, u32[]{:S(2)}) %collective-permute-start) | collective-permute-done | bytes 524320 | tf_op jit(solution)/shard_map/while/body/eval_jaxpr/ppermute | solution.py:10
  92.9 2.0 %gather_fusion = bf16[8,128,128]{2,1,0:T(8,128)(2,1)S(1)} fusion(bf16[2,2,12,128,128]{4,3,2,1,0:T(8,128)(2,1)} %get-tuple-element.347, s32[8]{0:T(128)S(1)} %reshape.102), kind=kCustom, calls=%fused_computation.clone.clone.1 | custom fusion | bytes 524384 | tf_op jit(solution)/shard_map/while/body/eval_jaxpr/jit(take_along_axis)/gather | solution.py:42
  94.9 3.4 %bitcast_add_fusion.3 = f32[2,2,128,1024]{3,2,1,0:T(8,128)} fusion(f32[2,2,128,1024]{3,2,1,0:T(8,128)} %get-tuple-element.331, bf16[2,128,1024,1,1]{2,1,0,4,3:T(8,128)(2,1)S(1)} %bitcast.71, pred[]{:T(512)S(6)} %compare.6, bf16[2,2,2,128,128]{4,3,2,1,0:T(8,128)(2,1)S(1)} %bitcast.72, pred[2,2,2]{2,1,0:T(4,128)(4,1)S(1)} %and_bitcast_fusion.3, ...), kind=kOutput, calls=%fused_computation.5.clone.1 | convolution fusion | flops 269746176 | bytes 4980753 | tf_op jit(solution)/shard_map/while/body/eval_jaxpr/ricab,cbh->riah/dot_general | solution.py:45
  98.4 5.2 %collective-permute-done = bf16[256,1024]{1,0:T(8,128)(2,1)S(1)} collective-permute-done((bf16[256,1024]{1,0:T(8,128)(2,1)S(1)}, bf16[256,1024]{1,0:T(8,128)(2,1)S(1)}, u32[]{:S(2)}, u32[]{:S(2)}) %collective-permute-start) | collective-permute-done | bytes 524320 | tf_op jit(solution)/shard_map/while/body/eval_jaxpr/ppermute | solution.py:10
  104.3 2.0 %gather_fusion = bf16[8,128,128]{2,1,0:T(8,128)(2,1)S(1)} fusion(bf16[2,2,12,128,128]{4,3,2,1,0:T(8,128)(2,1)} %get-tuple-element.347, s32[8]{0:T(128)S(1)} %reshape.102), kind=kCustom, calls=%fused_computation.clone.clone.1 | custom fusion | bytes 524384 | tf_op jit(solution)/shard_map/while/body/eval_jaxpr/jit(take_along_axis)/gather | solution.py:42
  106.3 3.4 %bitcast_add_fusion.3 = f32[2,2,128,1024]{3,2,1,0:T(8,128)} fusion(f32[2,2,128,1024]{3,2,1,0:T(8,128)} %get-tuple-element.331, bf16[2,128,1024,1,1]{2,1,0,4,3:T(8,128)(2,1)S(1)} %bitcast.71, pred[]{:T(512)S(6)} %compare.6, bf16[2,2,2,128,128]{4,3,2,1,0:T(8,128)(2,1)S(1)} %bitcast.72, pred[2,2,2]{2,1,0:T(4,128)(4,1)S(1)} %and_bitcast_fusion.3, ...), kind=kOutput, calls=%fused_computation.5.clone.1 | convolution fusion | flops 269746176 | bytes 4980753 | tf_op jit(solution)/shard_map/while/body/eval_jaxpr/ricab,cbh->riah/dot_general | solution.py:45
  109.7 5.2 %collective-permute-done = bf16[256,1024]{1,0:T(8,128)(2,1)S(1)} collective-permute-done((bf16[256,1024]{1,0:T(8,128)(2,1)S(1)}, bf16[256,1024]{1,0:T(8,128)(2,1)S(1)}, u32[]{:S(2)}, u32[]{:S(2)}) %collective-permute-start) | collective-permute-done | bytes 524320 | tf_op jit(solution)/shard_map/while/body/eval_jaxpr/ppermute | solution.py:10
  114.9 1.6 fusion.17
  116.6 1.7 bitcast_add_fusion.1
  119.0 1.8 fusion.27
  120.8 56.9 %all-reduce.2.cloned.1.call-done = f32[2,256,1024]{2,1,0:T(8,128)} async-done(((f32[2,256,1024]{2,1,0:T(8,128)}), f32[2,256,1024]{2,1,0:T(8,128)}) %all-reduce.2.cloned.1.call-update) | async-done | bytes 2097168 | tf_op jit(solution)/shard_map/psum | solution.py:63
  177.6 2.0 %divide_convert_fusion = bf16[2,256,1024]{2,1,0:T(8,128)(2,1)S(1)} fusion(f32[2,256,1024]{2,1,0:T(8,128)} %all-reduce.2.cloned.1.call-done, f32[2,256]{1,0:T(2,128)S(1)} %convert_element_type.15), kind=kLoop, calls=%fused_computation.23 | loop fusion | flops 1048576 | bytes 3147776 | tf_op jit(solution)/shard_map/convert.1
  181.4 1.5 fusion.16
  (89 shorter events, 10.2 us)
Async XLA Ops:
  6.5 112.4 %copy-start = (bf16[1024,1024]{1,0:T(8,128)(2,1)S(1)}, bf16[1024,1024]{1,0:T(8,128)(2,1)}, u32[]{:S(2)}) copy-start(bf16[1024,1024]{1,0:T(8,128)(2,1)} %param.17) | copy-start | bytes 6291460
  6.5 28.6 %copy-start.5 = (s32[2,2]{1,0:T(2,128)S(1)}, s32[2,2]{1,0:T(2,128)}, u32[]{:S(2)}) copy-start(s32[2,2]{1,0:T(2,128)} %param.15) | copy-start | bytes 52
  6.5 28.6 %copy-start.4 = (s32[2,2,12]{2,1,0:T(2,128)S(1)}, s32[2,2,12]{2,1,0:T(2,128)}, u32[]{:S(2)}) copy-start(s32[2,2,12]{2,1,0:T(2,128)} %param.14) | copy-start | bytes 580
  6.5 171.1 %all-reduce.2.cloned.1.call-start = ((), (), s32[]{:S(2)}) async-start(), calls=%async_computation | async-start | bytes 4194304 | tf_op jit(solution)/shard_map/psum | solution.py:63
  6.5 27.5 %collective-permute-start.1 = (bf16[256,1024]{1,0:T(8,128)(2,1)}, bf16[256,1024]{1,0:T(8,128)(2,1)S(1)}, u32[]{:S(2)}, u32[]{:S(2)}) collective-permute-start(bf16[256,1024]{1,0:T(8,128)(2,1)} %param.12), channel_id=1, source_target_pairs={{16,0},{18,2},{20,4},{22,6},{24,8},{26,10},{28,12},{30,14},{0,16},... | collective-permute-start | bytes 1572872 | tf_op jit(solution)/shard_map/ppermute | solution.py:10
  35.2 11.4 %collective-permute-start = (bf16[256,1024]{1,0:T(8,128)(2,1)S(1)}, bf16[256,1024]{1,0:T(8,128)(2,1)S(1)}, u32[]{:S(2)}, u32[]{:S(2)}) collective-permute-start(bf16[256,1024]{1,0:T(8,128)(2,1)S(1)} %copy.18), channel_id=1, source_target_pairs={{30,0},{0,2},{2,4},{4,6},{6,8},{8,10},{10,12},{12,14},{14,16},{16,... | collective-permute-start | bytes 1572872 | tf_op jit(solution)/shard_map/while/body/eval_jaxpr/ppermute | solution.py:10
  46.6 11.4 %collective-permute-start = (bf16[256,1024]{1,0:T(8,128)(2,1)S(1)}, bf16[256,1024]{1,0:T(8,128)(2,1)S(1)}, u32[]{:S(2)}, u32[]{:S(2)}) collective-permute-start(bf16[256,1024]{1,0:T(8,128)(2,1)S(1)} %copy.18), channel_id=1, source_target_pairs={{30,0},{0,2},{2,4},{4,6},{6,8},{8,10},{10,12},{12,14},{14,16},{16,... | collective-permute-start | bytes 1572872 | tf_op jit(solution)/shard_map/while/body/eval_jaxpr/ppermute | solution.py:10
  58.0 11.4 %collective-permute-start = (bf16[256,1024]{1,0:T(8,128)(2,1)S(1)}, bf16[256,1024]{1,0:T(8,128)(2,1)S(1)}, u32[]{:S(2)}, u32[]{:S(2)}) collective-permute-start(bf16[256,1024]{1,0:T(8,128)(2,1)S(1)} %copy.18), channel_id=1, source_target_pairs={{30,0},{0,2},{2,4},{4,6},{6,8},{8,10},{10,12},{12,14},{14,16},{16,... | collective-permute-start | bytes 1572872 | tf_op jit(solution)/shard_map/while/body/eval_jaxpr/ppermute | solution.py:10
  69.4 11.4 %collective-permute-start = (bf16[256,1024]{1,0:T(8,128)(2,1)S(1)}, bf16[256,1024]{1,0:T(8,128)(2,1)S(1)}, u32[]{:S(2)}, u32[]{:S(2)}) collective-permute-start(bf16[256,1024]{1,0:T(8,128)(2,1)S(1)} %copy.18), channel_id=1, source_target_pairs={{30,0},{0,2},{2,4},{4,6},{6,8},{8,10},{10,12},{12,14},{14,16},{16,... | collective-permute-start | bytes 1572872 | tf_op jit(solution)/shard_map/while/body/eval_jaxpr/ppermute | solution.py:10
  80.8 11.4 %collective-permute-start = (bf16[256,1024]{1,0:T(8,128)(2,1)S(1)}, bf16[256,1024]{1,0:T(8,128)(2,1)S(1)}, u32[]{:S(2)}, u32[]{:S(2)}) collective-permute-start(bf16[256,1024]{1,0:T(8,128)(2,1)S(1)} %copy.18), channel_id=1, source_target_pairs={{30,0},{0,2},{2,4},{4,6},{6,8},{8,10},{10,12},{12,14},{14,16},{16,... | collective-permute-start | bytes 1572872 | tf_op jit(solution)/shard_map/while/body/eval_jaxpr/ppermute | solution.py:10
  92.2 11.4 %collective-permute-start = (bf16[256,1024]{1,0:T(8,128)(2,1)S(1)}, bf16[256,1024]{1,0:T(8,128)(2,1)S(1)}, u32[]{:S(2)}, u32[]{:S(2)}) collective-permute-start(bf16[256,1024]{1,0:T(8,128)(2,1)S(1)} %copy.18), channel_id=1, source_target_pairs={{30,0},{0,2},{2,4},{4,6},{6,8},{8,10},{10,12},{12,14},{14,16},{16,... | collective-permute-start | bytes 1572872 | tf_op jit(solution)/shard_map/while/body/eval_jaxpr/ppermute | solution.py:10
  103.6 11.4 %collective-permute-start = (bf16[256,1024]{1,0:T(8,128)(2,1)S(1)}, bf16[256,1024]{1,0:T(8,128)(2,1)S(1)}, u32[]{:S(2)}, u32[]{:S(2)}) collective-permute-start(bf16[256,1024]{1,0:T(8,128)(2,1)S(1)} %copy.18), channel_id=1, source_target_pairs={{30,0},{0,2},{2,4},{4,6},{6,8},{8,10},{10,12},{12,14},{14,16},{16,... | collective-permute-start | bytes 1572872 | tf_op jit(solution)/shard_map/while/body/eval_jaxpr/ppermute | solution.py:10
  114.9 1.7 copy-start.1
  118.3 0.7 copy-start.6
  177.6 2.2 %copy-start.2 = (bf16[1024,1024]{1,0:T(8,128)(2,1)S(1)}, bf16[1024,1024]{1,0:T(8,128)(2,1)}, u32[]{:S(2)}) copy-start(bf16[1024,1024]{1,0:T(8,128)(2,1)} %param.18) | copy-start | bytes 6291460
  179.9 1.6 copy-start.3
Sparse Core Ops, SparseCore 0:
  118.4 59.1 all-reduce.1
where the time goes:
time: 191 us; the launch traced here: 190 us
  waiting for transfers between devices  113 us (59%)
  matrix products  28.1 us (15%)
  local copies, waits for them, and re-layouts  19.5 us (10%)
  between operations  13.5 us (7%)
  other arithmetic  11.1 us (6%)
  starting transfers between devices  4.51 us (2%)
    psum x1, waiting for transfers between devices, on_device(): summed = lax.psum(stacked, 'rep')  56.9 us
    ppermute x8, waiting for transfers between devices, from_behind(): return lax.ppermute(block, axis, route)  55.8 us
    dot_general x8, matrix products, absorb(): jnp.einsum('ricab,cbh->riah', chosen, panel_blocks, preferred_element_typ...  24 us
    gather x16, local copies, waits for them, and re-layouts, absorb(): chosen = jnp.take_along_axis(tiles, picks[:, :, :, None, None], axis=2)  17.5 us
    ppermute x8, starting transfers between devices, from_behind(): return lax.ppermute(block, axis, route)  4.51 us
  transfers between devices with their start and end apart: 9, of which 9 were waited for; matrix products, arithmetic and copies ran while one was open for 25% of the time, Pallas kernels for 0%

commit v1 on v0

--- a/solution.py
+++ b/solution.py
@@ -60,7 +60,7 @@
     running, feature_panel = lax.fori_loop(0, half_cycle - 1, advance, (running, feature_panel))
     running = absorb(running, feature_panel, (anchor - (half_cycle - 1)) % cycle_size)
     stacked = running.reshape(2, node_rows, feat_width)
-    summed = lax.psum(stacked, "rep")
+    summed = jnp.sum(jax.lax.all_gather(stacked, axis_name="rep"), 0)
     return finish(summed, degrees, features, w_self, w_in, w_out)
 
 

time: 191 us -> 189 us (0.990)
  waiting for transfers between devices: 113 us -> 107 us
  other arithmetic: 11.1 us -> 15.2 us
    psum x1 -> x0, waiting for transfers between devices: 56.9 us -> none  [on_device(): summed = lax.psum(stacked, 'rep')]
    all_gather x0 -> x1, waiting for transfers between devices: none -> 50.8 us  [on_device(): summed = jnp.sum(jax.lax.all_gather(stacked, axis_name='rep'), 0)]
    reduce_sum x0 -> x1, other arithmetic: none -> 4.12 us  [on_device(): summed = jnp.sum(jax.lax.all_gather(stacked, axis_name='rep'), 0)]
  transfers between devices with their start and end apart: 9 -> 9, of which waited for: 9 -> 9; matrix products, arithmetic and copies ran while one was open for 25% -> 26% of each run, Pallas kernels for 0% -> 0%
where the time goes in v1:
time: 189 us; the launch traced here: 188 us
  waiting for transfers between devices  107 us (57%)
  matrix products  28 us (15%)
  local copies, waits for them, and re-layouts  19.5 us (10%)
  other arithmetic  15.2 us (8%)
  between operations  13.5 us (7%)
  starting transfers between devices  4.51 us (2%)
    ppermute x8, waiting for transfers between devices, from_behind(): return lax.ppermute(block, axis, route)  55.8 us
    all_gather x1, waiting for transfers between devices, on_device(): summed = jnp.sum(jax.lax.all_gather(stacked, axis_name='rep'), 0)  50.8 us
    dot_general x8, matrix products, absorb(): jnp.einsum('ricab,cbh->riah', chosen, panel_blocks, preferred_element_typ...  24 us
    gather x16, local copies, waits for them, and re-layouts, absorb(): chosen = jnp.take_along_axis(tiles, picks[:, :, :, None, None], axis=2)  17.5 us
    ppermute x8, starting transfers between devices, from_behind(): return lax.ppermute(block, axis, route)  4.51 us
    reduce_sum x1, other arithmetic, on_device(): summed = jnp.sum(jax.lax.all_gather(stacked, axis_name='rep'), 0)  4.12 us
  transfers between devices with their start and end apart: 9, of which 9 were waited for; matrix products, arithmetic and copies ran while one was open for 26% of the time, Pallas kernels for 0%

profile of v1, /device:TPU:0, one launch (start us, length us, event | category | flops | bytes accessed | tf_op | source)
XLA Modules:
  0.0 187.8 jit_solution(18121934693025499640)
XLA Ops:
  6.5 4.1 %collective-permute-start.1 = (bf16[256,1024]{1,0:T(8,128)(2,1)}, bf16[256,1024]{1,0:T(8,128)(2,1)S(1)}, u32[]{:S(2)}, u32[]{:S(2)}) collective-permute-start(bf16[256,1024]{1,0:T(8,128)(2,1)} %param.12), channel_id=1, source_target_pairs={{16,0},{18,2},{20,4},{22,6},{24,8},{26,10},{28,12},{30,14},{0,16},... | collective-permute-start | bytes 1572872 | tf_op jit(solution)/shard_map/ppermute | solution.py:10
  12.4 2.7 %gather_fusion.1 = bf16[8,128,128]{2,1,0:T(8,128)(2,1)} fusion(bf16[2,2,12,128,128]{4,3,2,1,0:T(8,128)(2,1)} %param.13, s32[8]{0:T(128)S(1)} %reshape.85), kind=kCustom, calls=%fused_computation.1.clone | custom fusion | bytes 524384 | tf_op jit(solution)/shard_map/jit(take_along_axis)/gather | solution.py:42
  16.0 18.0 %collective-permute-done.1 = bf16[256,1024]{1,0:T(8,128)(2,1)S(1)} collective-permute-done((bf16[256,1024]{1,0:T(8,128)(2,1)}, bf16[256,1024]{1,0:T(8,128)(2,1)S(1)}, u32[]{:S(2)}, u32[]{:S(2)}) %collective-permute-start.1) | collective-permute-done | bytes 524320 | tf_op jit(solution)/shard_map/ppermute | solution.py:10
  35.1 79.8 %while.18 = (s32[]{:T(128)}, f32[2,2,128,1024]{3,2,1,0:T(8,128)}, bf16[256,1024]{1,0:T(8,128)(2,1)S(1)}, s32[2,2,12]{2,1,0:T(2,128)S(1)}, s32[]{:T(128)}, /*inde...) while((s32[]{:T(128)}, f32[2,2,128,1024]{3,2,1,0:T(8,128)}, ...), condition=%wide.region_3.5_spmd.clone, body=%wide.region_0.4_spmd.clone.sunk | while | flops 269747040 | bytes 8651944 | solution.py:60
  35.9 2.0 %gather_fusion = bf16[8,128,128]{2,1,0:T(8,128)(2,1)S(1)} fusion(bf16[2,2,12,128,128]{4,3,2,1,0:T(8,128)(2,1)} %get-tuple-element.347, s32[8]{0:T(128)S(1)} %reshape.98), kind=kCustom, calls=%fused_computation.clone.clone.1 | custom fusion | bytes 524384 | tf_op jit(solution)/shard_map/while/body/eval_jaxpr/jit(take_along_axis)/gather | solution.py:42
  37.9 1.8 bitcast_add_fusion.3
  39.8 6.8 %collective-permute-done = bf16[256,1024]{1,0:T(8,128)(2,1)S(1)} collective-permute-done((bf16[256,1024]{1,0:T(8,128)(2,1)S(1)}, bf16[256,1024]{1,0:T(8,128)(2,1)S(1)}, u32[]{:S(2)}, u32[]{:S(2)}) %collective-permute-start) | collective-permute-done | bytes 524320 | tf_op jit(solution)/shard_map/while/body/eval_jaxpr/ppermute | solution.py:10
  47.3 2.0 %gather_fusion = bf16[8,128,128]{2,1,0:T(8,128)(2,1)S(1)} fusion(bf16[2,2,12,128,128]{4,3,2,1,0:T(8,128)(2,1)} %get-tuple-element.347, s32[8]{0:T(128)S(1)} %reshape.98), kind=kCustom, calls=%fused_computation.clone.clone.1 | custom fusion | bytes 524384 | tf_op jit(solution)/shard_map/while/body/eval_jaxpr/jit(take_along_axis)/gather | solution.py:42
  49.3 3.4 %bitcast_add_fusion.3 = f32[2,2,128,1024]{3,2,1,0:T(8,128)} fusion(f32[2,2,128,1024]{3,2,1,0:T(8,128)} %get-tuple-element.331, bf16[2,128,1024,1,1]{2,1,0,4,3:T(8,128)(2,1)S(1)} %bitcast.71, pred[]{:T(512)S(6)} %compare.6, bf16[2,2,2,128,128]{4,3,2,1,0:T(8,128)(2,1)S(1)} %bitcast.72, pred[2,2,2]{2,1,0:T(4,128)(4,1)S(1)} %and_bitcast_fusion.3, ...), kind=kOutput, calls=%fused_computation.5.clone.1 | convolution fusion | flops 269746176 | bytes 4980753 | tf_op jit(solution)/shard_map/while/body/eval_jaxpr/ricab,cbh->riah/dot_general | solution.py:45
  52.8 5.2 %collective-permute-done = bf16[256,1024]{1,0:T(8,128)(2,1)S(1)} collective-permute-done((bf16[256,1024]{1,0:T(8,128)(2,1)S(1)}, bf16[256,1024]{1,0:T(8,128)(2,1)S(1)}, u32[]{:S(2)}, u32[]{:S(2)}) %collective-permute-start) | collective-permute-done | bytes 524320 | tf_op jit(solution)/shard_map/while/body/eval_jaxpr/ppermute | solution.py:10
  58.7 2.0 %gather_fusion = bf16[8,128,128]{2,1,0:T(8,128)(2,1)S(1)} fusion(bf16[2,2,12,128,128]{4,3,2,1,0:T(8,128)(2,1)} %get-tuple-element.347, s32[8]{0:T(128)S(1)} %reshape.98), kind=kCustom, calls=%fused_computation.clone.clone.1 | custom fusion | bytes 524384 | tf_op jit(solution)/shard_map/while/body/eval_jaxpr/jit(take_along_axis)/gather | solution.py:42
  60.7 3.4 %bitcast_add_fusion.3 = f32[2,2,128,1024]{3,2,1,0:T(8,128)} fusion(f32[2,2,128,1024]{3,2,1,0:T(8,128)} %get-tuple-element.331, bf16[2,128,1024,1,1]{2,1,0,4,3:T(8,128)(2,1)S(1)} %bitcast.71, pred[]{:T(512)S(6)} %compare.6, bf16[2,2,2,128,128]{4,3,2,1,0:T(8,128)(2,1)S(1)} %bitcast.72, pred[2,2,2]{2,1,0:T(4,128)(4,1)S(1)} %and_bitcast_fusion.3, ...), kind=kOutput, calls=%fused_computation.5.clone.1 | convolution fusion | flops 269746176 | bytes 4980753 | tf_op jit(solution)/shard_map/while/body/eval_jaxpr/ricab,cbh->riah/dot_general | solution.py:45
  64.2 5.2 %collective-permute-done = bf16[256,1024]{1,0:T(8,128)(2,1)S(1)} collective-permute-done((bf16[256,1024]{1,0:T(8,128)(2,1)S(1)}, bf16[256,1024]{1,0:T(8,128)(2,1)S(1)}, u32[]{:S(2)}, u32[]{:S(2)}) %collective-permute-start) | collective-permute-done | bytes 524320 | tf_op jit(solution)/shard_map/while/body/eval_jaxpr/ppermute | solution.py:10
  70.1 2.0 %gather_fusion = bf16[8,128,128]{2,1,0:T(8,128)(2,1)S(1)} fusion(bf16[2,2,12,128,128]{4,3,2,1,0:T(8,128)(2,1)} %get-tuple-element.347, s32[8]{0:T(128)S(1)} %reshape.98), kind=kCustom, calls=%fused_computation.clone.clone.1 | custom fusion | bytes 524384 | tf_op jit(solution)/shard_map/while/body/eval_jaxpr/jit(take_along_axis)/gather | solution.py:42
  72.1 3.4 %bitcast_add_fusion.3 = f32[2,2,128,1024]{3,2,1,0:T(8,128)} fusion(f32[2,2,128,1024]{3,2,1,0:T(8,128)} %get-tuple-element.331, bf16[2,128,1024,1,1]{2,1,0,4,3:T(8,128)(2,1)S(1)} %bitcast.71, pred[]{:T(512)S(6)} %compare.6, bf16[2,2,2,128,128]{4,3,2,1,0:T(8,128)(2,1)S(1)} %bitcast.72, pred[2,2,2]{2,1,0:T(4,128)(4,1)S(1)} %and_bitcast_fusion.3, ...), kind=kOutput, calls=%fused_computation.5.clone.1 | convolution fusion | flops 269746176 | bytes 4980753 | tf_op jit(solution)/shard_map/while/body/eval_jaxpr/ricab,cbh->riah/dot_general | solution.py:45
  75.6 5.2 %collective-permute-done = bf16[256,1024]{1,0:T(8,128)(2,1)S(1)} collective-permute-done((bf16[256,1024]{1,0:T(8,128)(2,1)S(1)}, bf16[256,1024]{1,0:T(8,128)(2,1)S(1)}, u32[]{:S(2)}, u32[]{:S(2)}) %collective-permute-start) | collective-permute-done | bytes 524320 | tf_op jit(solution)/shard_map/while/body/eval_jaxpr/ppermute | solution.py:10
  81.5 2.0 %gather_fusion = bf16[8,128,128]{2,1,0:T(8,128)(2,1)S(1)} fusion(bf16[2,2,12,128,128]{4,3,2,1,0:T(8,128)(2,1)} %get-tuple-element.347, s32[8]{0:T(128)S(1)} %reshape.98), kind=kCustom, calls=%fused_computation.clone.clone.1 | custom fusion | bytes 524384 | tf_op jit(solution)/shard_map/while/body/eval_jaxpr/jit(take_along_axis)/gather | solution.py:42
  83.5 3.4 %bitcast_add_fusion.3 = f32[2,2,128,1024]{3,2,1,0:T(8,128)} fusion(f32[2,2,128,1024]{3,2,1,0:T(8,128)} %get-tuple-element.331, bf16[2,128,1024,1,1]{2,1,0,4,3:T(8,128)(2,1)S(1)} %bitcast.71, pred[]{:T(512)S(6)} %compare.6, bf16[2,2,2,128,128]{4,3,2,1,0:T(8,128)(2,1)S(1)} %bitcast.72, pred[2,2,2]{2,1,0:T(4,128)(4,1)S(1)} %and_bitcast_fusion.3, ...), kind=kOutput, calls=%fused_computation.5.clone.1 | convolution fusion | flops 269746176 | bytes 4980753 | tf_op jit(solution)/shard_map/while/body/eval_jaxpr/ricab,cbh->riah/dot_general | solution.py:45
  87.0 5.2 %collective-permute-done = bf16[256,1024]{1,0:T(8,128)(2,1)S(1)} collective-permute-done((bf16[256,1024]{1,0:T(8,128)(2,1)S(1)}, bf16[256,1024]{1,0:T(8,128)(2,1)S(1)}, u32[]{:S(2)}, u32[]{:S(2)}) %collective-permute-start) | collective-permute-done | bytes 524320 | tf_op jit(solution)/shard_map/while/body/eval_jaxpr/ppermute | solution.py:10
  92.9 2.0 %gather_fusion = bf16[8,128,128]{2,1,0:T(8,128)(2,1)S(1)} fusion(bf16[2,2,12,128,128]{4,3,2,1,0:T(8,128)(2,1)} %get-tuple-element.347, s32[8]{0:T(128)S(1)} %reshape.98), kind=kCustom, calls=%fused_computation.clone.clone.1 | custom fusion | bytes 524384 | tf_op jit(solution)/shard_map/while/body/eval_jaxpr/jit(take_along_axis)/gather | solution.py:42
  94.9 3.4 %bitcast_add_fusion.3 = f32[2,2,128,1024]{3,2,1,0:T(8,128)} fusion(f32[2,2,128,1024]{3,2,1,0:T(8,128)} %get-tuple-element.331, bf16[2,128,1024,1,1]{2,1,0,4,3:T(8,128)(2,1)S(1)} %bitcast.71, pred[]{:T(512)S(6)} %compare.6, bf16[2,2,2,128,128]{4,3,2,1,0:T(8,128)(2,1)S(1)} %bitcast.72, pred[2,2,2]{2,1,0:T(4,128)(4,1)S(1)} %and_bitcast_fusion.3, ...), kind=kOutput, calls=%fused_computation.5.clone.1 | convolution fusion | flops 269746176 | bytes 4980753 | tf_op jit(solution)/shard_map/while/body/eval_jaxpr/ricab,cbh->riah/dot_general | solution.py:45
  98.4 5.2 %collective-permute-done = bf16[256,1024]{1,0:T(8,128)(2,1)S(1)} collective-permute-done((bf16[256,1024]{1,0:T(8,128)(2,1)S(1)}, bf16[256,1024]{1,0:T(8,128)(2,1)S(1)}, u32[]{:S(2)}, u32[]{:S(2)}) %collective-permute-start) | collective-permute-done | bytes 524320 | tf_op jit(solution)/shard_map/while/body/eval_jaxpr/ppermute | solution.py:10
  104.3 2.0 %gather_fusion = bf16[8,128,128]{2,1,0:T(8,128)(2,1)S(1)} fusion(bf16[2,2,12,128,128]{4,3,2,1,0:T(8,128)(2,1)} %get-tuple-element.347, s32[8]{0:T(128)S(1)} %reshape.98), kind=kCustom, calls=%fused_computation.clone.clone.1 | custom fusion | bytes 524384 | tf_op jit(solution)/shard_map/while/body/eval_jaxpr/jit(take_along_axis)/gather | solution.py:42
  106.3 3.4 %bitcast_add_fusion.3 = f32[2,2,128,1024]{3,2,1,0:T(8,128)} fusion(f32[2,2,128,1024]{3,2,1,0:T(8,128)} %get-tuple-element.331, bf16[2,128,1024,1,1]{2,1,0,4,3:T(8,128)(2,1)S(1)} %bitcast.71, pred[]{:T(512)S(6)} %compare.6, bf16[2,2,2,128,128]{4,3,2,1,0:T(8,128)(2,1)S(1)} %bitcast.72, pred[2,2,2]{2,1,0:T(4,128)(4,1)S(1)} %and_bitcast_fusion.3, ...), kind=kOutput, calls=%fused_computation.5.clone.1 | convolution fusion | flops 269746176 | bytes 4980753 | tf_op jit(solution)/shard_map/while/body/eval_jaxpr/ricab,cbh->riah/dot_general | solution.py:45
  109.7 5.2 %collective-permute-done = bf16[256,1024]{1,0:T(8,128)(2,1)S(1)} collective-permute-done((bf16[256,1024]{1,0:T(8,128)(2,1)S(1)}, bf16[256,1024]{1,0:T(8,128)(2,1)S(1)}, u32[]{:S(2)}, u32[]{:S(2)}) %collective-permute-start) | collective-permute-done | bytes 524320 | tf_op jit(solution)/shard_map/while/body/eval_jaxpr/ppermute | solution.py:10
  114.9 1.6 fusion.17
  116.6 1.7 bitcast_add_fusion.1
  119.0 1.7 fusion.27
  120.8 50.8 %all-gather.2.cloned.1.call-done = f32[2,2,256,1024]{3,2,1,0:T(8,128)} async-done(((f32[1,2,256,1024]{3,2,1,0:T(8,128)}), f32[2,2,256,1024]{3,2,1,0:T(8,128)}) %all-gather.2.cloned.1.call-update) | async-done | bytes 4194320 | tf_op jit(solution)/shard_map/all_gather | solution.py:63
  171.5 4.1 %reduce_sum.35 = f32[2,256,1024]{2,1,0:T(8,128)} reduce(f32[2,2,256,1024]{3,2,1,0:T(8,128)} %all-gather.2.cloned.1.call-done, f32[]{:T(128)} %constant.110.clone.1), dimensions={0}, to_apply=%region_6.8 | reduce | flops 524288 | bytes 6291460 | tf_op jit(solution)/shard_map/reduce_sum | solution.py:63
  175.6 2.0 %divide_convert_fusion = bf16[2,256,1024]{2,1,0:T(8,128)(2,1)S(1)} fusion(f32[2,256,1024]{2,1,0:T(8,128)} %reduce_sum.35, f32[2,256]{1,0:T(2,128)S(1)} %convert_element_type.15), kind=kLoop, calls=%fused_computation.23 | loop fusion | flops 1048576 | bytes 3147776 | tf_op jit(solution)/shard_map/convert.1
  179.4 1.5 fusion.16
  (90 shorter events, 11.3 us)
Async XLA Ops:
  6.5 112.5 %copy-start = (bf16[1024,1024]{1,0:T(8,128)(2,1)S(1)}, bf16[1024,1024]{1,0:T(8,128)(2,1)}, u32[]{:S(2)}) copy-start(bf16[1024,1024]{1,0:T(8,128)(2,1)} %param.17) | copy-start | bytes 6291460
  6.5 28.6 %copy-start.5 = (s32[2,2]{1,0:T(2,128)S(1)}, s32[2,2]{1,0:T(2,128)}, u32[]{:S(2)}) copy-start(s32[2,2]{1,0:T(2,128)} %param.15) | copy-start | bytes 52
  6.5 28.6 %copy-start.4 = (s32[2,2,12]{2,1,0:T(2,128)S(1)}, s32[2,2,12]{2,1,0:T(2,128)}, u32[]{:S(2)}) copy-start(s32[2,2,12]{2,1,0:T(2,128)} %param.14) | copy-start | bytes 580
  6.5 165.0 %all-gather.2.cloned.1.call-start = ((), (), s32[]{:S(2)}) async-start(), calls=%async_computation | async-start | bytes 6291456 | tf_op jit(solution)/shard_map/all_gather | solution.py:63
  6.5 27.5 %collective-permute-start.1 = (bf16[256,1024]{1,0:T(8,128)(2,1)}, bf16[256,1024]{1,0:T(8,128)(2,1)S(1)}, u32[]{:S(2)}, u32[]{:S(2)}) collective-permute-start(bf16[256,1024]{1,0:T(8,128)(2,1)} %param.12), channel_id=1, source_target_pairs={{16,0},{18,2},{20,4},{22,6},{24,8},{26,10},{28,12},{30,14},{0,16},... | collective-permute-start | bytes 1572872 | tf_op jit(solution)/shard_map/ppermute | solution.py:10
  35.2 11.4 %collective-permute-start = (bf16[256,1024]{1,0:T(8,128)(2,1)S(1)}, bf16[256,1024]{1,0:T(8,128)(2,1)S(1)}, u32[]{:S(2)}, u32[]{:S(2)}) collective-permute-start(bf16[256,1024]{1,0:T(8,128)(2,1)S(1)} %copy.18), channel_id=1, source_target_pairs={{30,0},{0,2},{2,4},{4,6},{6,8},{8,10},{10,12},{12,14},{14,16},{16,... | collective-permute-start | bytes 1572872 | tf_op jit(solution)/shard_map/while/body/eval_jaxpr/ppermute | solution.py:10
  46.6 11.4 %collective-permute-start = (bf16[256,1024]{1,0:T(8,128)(2,1)S(1)}, bf16[256,1024]{1,0:T(8,128)(2,1)S(1)}, u32[]{:S(2)}, u32[]{:S(2)}) collective-permute-start(bf16[256,1024]{1,0:T(8,128)(2,1)S(1)} %copy.18), channel_id=1, source_target_pairs={{30,0},{0,2},{2,4},{4,6},{6,8},{8,10},{10,12},{12,14},{14,16},{16,... | collective-permute-start | bytes 1572872 | tf_op jit(solution)/shard_map/while/body/eval_jaxpr/ppermute | solution.py:10
  58.0 11.4 %collective-permute-start = (bf16[256,1024]{1,0:T(8,128)(2,1)S(1)}, bf16[256,1024]{1,0:T(8,128)(2,1)S(1)}, u32[]{:S(2)}, u32[]{:S(2)}) collective-permute-start(bf16[256,1024]{1,0:T(8,128)(2,1)S(1)} %copy.18), channel_id=1, source_target_pairs={{30,0},{0,2},{2,4},{4,6},{6,8},{8,10},{10,12},{12,14},{14,16},{16,... | collective-permute-start | bytes 1572872 | tf_op jit(solution)/shard_map/while/body/eval_jaxpr/ppermute | solution.py:10
  69.4 11.4 %collective-permute-start = (bf16[256,1024]{1,0:T(8,128)(2,1)S(1)}, bf16[256,1024]{1,0:T(8,128)(2,1)S(1)}, u32[]{:S(2)}, u32[]{:S(2)}) collective-permute-start(bf16[256,1024]{1,0:T(8,128)(2,1)S(1)} %copy.18), channel_id=1, source_target_pairs={{30,0},{0,2},{2,4},{4,6},{6,8},{8,10},{10,12},{12,14},{14,16},{16,... | collective-permute-start | bytes 1572872 | tf_op jit(solution)/shard_map/while/body/eval_jaxpr/ppermute | solution.py:10
  80.8 11.4 %collective-permute-start = (bf16[256,1024]{1,0:T(8,128)(2,1)S(1)}, bf16[256,1024]{1,0:T(8,128)(2,1)S(1)}, u32[]{:S(2)}, u32[]{:S(2)}) collective-permute-start(bf16[256,1024]{1,0:T(8,128)(2,1)S(1)} %copy.18), channel_id=1, source_target_pairs={{30,0},{0,2},{2,4},{4,6},{6,8},{8,10},{10,12},{12,14},{14,16},{16,... | collective-permute-start | bytes 1572872 | tf_op jit(solution)/shard_map/while/body/eval_jaxpr/ppermute | solution.py:10
  92.2 11.4 %collective-permute-start = (bf16[256,1024]{1,0:T(8,128)(2,1)S(1)}, bf16[256,1024]{1,0:T(8,128)(2,1)S(1)}, u32[]{:S(2)}, u32[]{:S(2)}) collective-permute-start(bf16[256,1024]{1,0:T(8,128)(2,1)S(1)} %copy.18), channel_id=1, source_target_pairs={{30,0},{0,2},{2,4},{4,6},{6,8},{8,10},{10,12},{12,14},{14,16},{16,... | collective-permute-start | bytes 1572872 | tf_op jit(solution)/shard_map/while/body/eval_jaxpr/ppermute | solution.py:10
  103.6 11.4 %collective-permute-start = (bf16[256,1024]{1,0:T(8,128)(2,1)S(1)}, bf16[256,1024]{1,0:T(8,128)(2,1)S(1)}, u32[]{:S(2)}, u32[]{:S(2)}) collective-permute-start(bf16[256,1024]{1,0:T(8,128)(2,1)S(1)} %copy.18), channel_id=1, source_target_pairs={{30,0},{0,2},{2,4},{4,6},{6,8},{8,10},{10,12},{12,14},{14,16},{16,... | collective-permute-start | bytes 1572872 | tf_op jit(solution)/shard_map/while/body/eval_jaxpr/ppermute | solution.py:10
  114.9 1.7 copy-start.1
  118.3 0.7 copy-start.6
  175.6 2.2 %copy-start.2 = (bf16[1024,1024]{1,0:T(8,128)(2,1)S(1)}, bf16[1024,1024]{1,0:T(8,128)(2,1)}, u32[]{:S(2)}) copy-start(bf16[1024,1024]{1,0:T(8,128)(2,1)} %param.18) | copy-start | bytes 6291460
  177.8 1.6 copy-start.3
Sparse Core Ops, SparseCore 0:
  118.5 52.9 all-gather.1
